TPU v7x, 32 devices: a whole 2x2x4 slice. The times are simulated.
32 devices in a mesh: row: 16 (over z, y, x), col: 2 (over core).
Axes of the slice: x: 2, y: 2, z: 4, core: 2. Of those that a mesh axis runs over, the one named last changes fastest.
Arguments:
- acts: bfloat16 [2048, 8192], P('row'), may hold values from -22 to 22
- out_grads: bfloat16 [2048, 4096], P('row', 'col'), may hold values from -0.198873782 to 0.198873782
- weight: float32 [8192, 4096], P('row', 'col'), may hold values from -30 to 30
- row_state: float32 [8192], P('row'), may hold values from 0.002 to 2
- col_state: float32 [4096], P('col'), may hold values from 0.01 to 0.3
Outputs:
- new_weight: float32 [8192, 4096], P('row', 'col')
- update: float32 [8192, 4096], P('row', 'col')
- row_moment: float32 [8192], P('row')
- col_moment: float32 [4096], P('col')
All inputs are finite; a program needn't handle non-finite values.
Results may differ from a plain program's by a relative error of at most 0.0003.
Values may be sent and summed in bfloat16 or wider, within the bound.
No kernel may reach another device: no remote copies, remote signals or barrier semaphores. Data moves between devices by JAX's collectives and lax.ppermute only.
A program may use at most 64 MiB of HBM per device.

v0:
```python
import jax
import jax.numpy as jnp
from jax import lax
from jax.sharding import PartitionSpec as P

decay_rate = 0.85
floor_eps = 1e-30
relative_rate = 0.05


def per_device(acts, out_grads, weight, row_state, col_state):
    n_col = lax.axis_size("col")
    width = acts.shape[1]
    cols_here = out_grads.shape[1]
    cols_all = cols_here * n_col
    columns = lax.all_to_all(acts, "row", split_axis=1, concat_axis=0, tiled=True)
    gradient = lax.dot_general(
        columns,
        lax.all_gather(out_grads, "row", axis=0, tiled=True),
        (((0,), (0,)), ((), ())),
        preferred_element_type=jnp.float32,
    )
    squares = gradient * gradient + floor_eps
    row_squares = jnp.sum(squares, axis=1)
    col_squares = jnp.sum(squares, axis=0)
    weight_part = jnp.sum(weight * weight)
    row_total = lax.psum(row_squares, "col")
    col_total = lax.psum(col_squares, "row")
    weight_total = lax.psum(weight_part, ("row", "col"))
    row_moment = decay_rate * row_state + (1.0 - decay_rate) * (row_total / cols_all)
    col_moment = decay_rate * col_state + (1.0 - decay_rate) * (col_total / width)
    unclipped = gradient * lax.rsqrt(row_moment[:, None] * col_moment[None, :])
    update_total = lax.psum(jnp.sum(unclipped * unclipped), ("row", "col"))
    count_all = width * cols_all
    clip_factor = jnp.maximum(1.0, jnp.sqrt(update_total / count_all))
    update = unclipped / clip_factor
    step_size = relative_rate * jnp.sqrt(weight_total / count_all + 1e-06)
    new_weight = weight - step_size * update
    return (new_weight, update, row_moment, col_moment)


def solution(mesh):
    return jax.shard_map(
        per_device,
        mesh=mesh,
        in_specs=(P("row", None), P("row", "col"), P("row", "col"), P("row"), P("col")),
        out_specs=(P("row", "col"), P("row", "col"), P("row"), P("col")),
        check_vma=False,
    )
```

profile of v0, /device:TPU:12, one launch (start us, length us, event | category | flops | bytes accessed | tf_op | source)
XLA Modules:
  0.0 269.7 jit_solution(2994545322753481755)
XLA Ops:
  7.2 0.0 all-gather.2.cloned.1.call-start
  7.2 0.7 all-gather.2.cloned.1.call-update
  7.9 4.1 %copy.9 = bf16[128,8192]{0,1:T(8,128)(2,1)} copy(bf16[128,8192]{1,0:T(8,128)(2,1)} %param.5) | data formatting | bytes 4194304 | tf_op args[0]
  12.0 7.2 %all-to-all-start = ((bf16[128,16,512]{0,2,1:T(8,128)(2,1)}), bf16[128,16,512]{0,2,1:T(8,128)(2,1)S(1)}, u32[]{:S(2)}, u32[]{:S(2)}) async-start(bf16[128,16,512]{0,2,1:T(8,128)(2,1)} %bitcast.6), calls=%async_computation | async-start | bytes 4194304 | tf_op jit(solution)/shard_map/all_to_all | solution.py:16
  19.1 4.1 %multiply_reduce_fusion.1 = f32[]{:T(128)} fusion(f32[512,2048]{1,0:T(8,128)} %param.7), kind=kLoop, calls=%fused_computation.4 | loop fusion | flops 2097151 | bytes 4194308 | tf_op jit(solution)/shard_map/reduce_sum | solution.py:26
  23.3 77.5 %all-to-all-done = bf16[128,16,512]{0,2,1:T(8,128)(2,1)S(1)} async-done(((bf16[128,16,512]{0,2,1:T(8,128)(2,1)}), bf16[128,16,512]{0,2,1:T(8,128)(2,1)S(1)}, u32[]{:S(2)}, u32[]{:S(2)}) %all-to-all-start) | async-done | bytes 2097184 | tf_op jit(solution)/shard_map/all_to_all | solution.py:16
  100.7 2.6 copy.10
  103.3 52.0 %all-gather.2.cloned.1.call-done = bf16[2048,2048]{1,0:T(8,128)(2,1)} async-done(((bf16[128,2048]{1,0:T(8,128)(2,1)}), bf16[2048,2048]{1,0:T(8,128)(2,1)}) %all-gather.2.cloned.1.call-update) | async-done | bytes 8388624 | tf_op jit(solution)/shard_map/all_gather | solution.py:19
  155.4 0.0 copy-start.2
  155.4 0.0 copy-start.3
  155.4 10.9 %fusion.1 = (f32[512]{0:T(512)S(1)}, f32[2048]{0:T(1024)S(1)}, f32[512,2048]{1,0:T(8,128)}) fusion(bf16[2048,512]{1,0:T(8,128)(2,1)} %bitcast.7, bf16[2048,2048]{1,0:T(8,128)(2,1)} %all-gather.2.cloned.1.call-done), kind=kOutput, calls=%fused_computation.6 | convolution fusion | flops 4299159040 | bytes 14690304 | tf_op jit(solution)/shard_map/dot_general | solution.py:17
  166.3 30.4 %psum.30 = f32[2048]{0:T(1024)S(1)} all-reduce(f32[2048]{0:T(1024)S(1)} %get-tuple-element.5), channel_id=1, replica_groups=mesh['row'=16,'col'=2] {'row'}, use_global_device_ids=true, to_apply=%region_5.0 | all-reduce | flops 2048 | bytes 16384 | tf_op jit(solution)/shard_map/psum | solution.py:28
  196.7 2.5 psum.29
  199.2 0.0 copy-done.2
  199.2 0.0 copy-done.3
  199.2 0.0 copy-start
  199.2 0.0 copy-start.1
  199.2 4.1 %multiply_reduce_fusion = f32[]{:T(128)} fusion(f32[512,2048]{1,0:T(8,128)} %get-tuple-element.10, f32[2048]{0:T(1024)S(1)} %multiply_add_fusion.1, f32[512]{0:T(512)S(1)} %multiply_add_fusion.2), kind=kLoop, calls=%fused_computation.1 | loop fusion | flops 4194303 | bytes 4204548 | tf_op jit(solution)/shard_map/reduce_sum | solution.py:33
  203.3 49.3 %all-reduce = (f32[]{:T(128)}, f32[]{:T(128)}) all-reduce(f32[]{:T(128)} %multiply_reduce_fusion, f32[]{:T(128)} %multiply_reduce_fusion.1), channel_id=1, replica_groups=mesh['row'=16,'col'=2] {'row','col'}, use_global_device_ids=true, to_apply=%region_7.0 | all-reduce | flops 2 | bytes 16 | tf_op jit(solution)/shard_map/psum | solution.py:33
  253.9 8.9 %multiply_subtract_fusion = (f32[512,2048]{1,0:T(8,128)}, f32[512,2048]{1,0:T(8,128)}) fusion(f32[512,2048]{1,0:T(8,128)} %param.7, f32[]{:T(128)S(6)} %mul_shard_map.3, f32[]{:T(128)S(6)} %max_shard_map.3, f32[512,2048]{1,0:T(8,128)} %get-tuple-element.10, f32[2048]{0:T(1024)S(1)} %multiply_add_fusion.1, f32[512]{0:T(512)S(1)} %multiply_add_fusion.2), kind=kLoop, calls=%fused_computation | loop fusion | flops 5242880 | bytes 16787464 | tf_op jit(solution)/shard_map/sub | solution.py:38
  262.9 0.0 copy-done
  262.9 0.0 copy-done.1
  (2 shorter events, 0.0 us)
Async XLA Ops:
  7.2 148.2 %all-gather.2.cloned.1.call-start = ((), (), s32[]{:S(2)}) async-start(), calls=%async_computation.1 | async-start | bytes 8912896 | tf_op jit(solution)/shard_map/all_gather | solution.py:19
  12.0 88.8 %all-to-all-start = ((bf16[128,16,512]{0,2,1:T(8,128)(2,1)}), bf16[128,16,512]{0,2,1:T(8,128)(2,1)S(1)}, u32[]{:S(2)}, u32[]{:S(2)}) async-start(bf16[128,16,512]{0,2,1:T(8,128)(2,1)} %bitcast.6), calls=%async_computation | async-start | bytes 4194304 | tf_op jit(solution)/shard_map/all_to_all | solution.py:16
  155.4 43.8 %copy-start.2 = (f32[2048]{0:T(1024)S(1)}, f32[2048]{0:T(1024)}, u32[]{:S(2)}) copy-start(f32[2048]{0:T(1024)} %param.9) | copy-start | bytes 24580
  155.4 43.8 %copy-start.3 = (f32[512]{0:T(512)S(1)}, f32[512]{0:T(512)}, u32[]{:S(2)}) copy-start(f32[512]{0:T(512)} %param.8) | copy-start | bytes 6148
  199.2 63.7 %copy-start = (f32[2048]{0:T(1024)}, f32[2048]{0:T(1024)S(1)}, u32[]{:S(2)}) copy-start(f32[2048]{0:T(1024)S(1)} %multiply_add_fusion.1) | copy-start | bytes 24580
  199.2 63.6 %copy-start.1 = (f32[512]{0:T(512)}, f32[512]{0:T(512)S(1)}, u32[]{:S(2)}) copy-start(f32[512]{0:T(512)S(1)} %multiply_add_fusion.2) | copy-start | bytes 6148
Sparse Core Ops, SparseCore 0:
  10.7 144.5 all-gather.1
where the time goes:
time: 270 us
  waiting for transfers between devices  130 us (48%)
  blocking collectives  82.2 us (30%)
  other arithmetic  17.1 us (6%)
  between operations  15.4 us (6%)
  matrix products  10.9 us (4%)
  starting transfers between devices  7.21 us (3%)
  local copies, waits for them, and re-layouts  6.67 us (2%)
    all_to_all x1, waiting for transfers between devices, per_device(): lax.all_to_all(acts, 'row', split_axis=1, concat_axis=0, tiled=True)  77.5 us
    all_gather x1, waiting for transfers between devices, per_device(): lax.all_gather(out_grads, 'row', axis=0, tiled=True)  52 us
    psum x1, blocking collectives, per_device(): update_total = lax.psum(jnp.sum(unclipped * unclipped), ('row', 'col'))  49.3 us
    psum x1, blocking collectives, per_device(): col_total = lax.psum(col_squares, 'row')  30.4 us
    dot_general x1, matrix products, per_device(): lax.dot_general(columns, lax.all_gather(out_grads, 'row', axis=0, tiled=T...  10.9 us
    sub x1, other arithmetic, per_device(): new_weight = weight - step_size * update  8.93 us
    all_to_all x1, starting transfers between devices, per_device(): lax.all_to_all(acts, 'row', split_axis=1, concat_axis=0, tiled=True)  7.17 us
  transfers between devices with their start and end apart: 2, of which 2 were waited for; matrix products, arithmetic and copies ran while one was open for 4% of the time, Pallas kernels for 0%

commit v1 on v0

--- a/solution.py
+++ b/solution.py
@@ -2,6 +2,7 @@
 import jax.numpy as jnp
 from jax import lax
 from jax.sharding import PartitionSpec as P
+from jax.lax import all_to_all, axis_size
 
 decay_rate = 0.85
 floor_eps = 1e-30
@@ -13,7 +14,15 @@
     width = acts.shape[1]
     cols_here = out_grads.shape[1]
     cols_all = cols_here * n_col
-    columns = lax.all_to_all(acts, "row", split_axis=1, concat_axis=0, tiled=True)
+    columns = jnp.concatenate(
+        all_to_all(
+            jnp.stack(jnp.split(acts, axis_size("row"), axis=1), axis=0),
+            axis_name="row",
+            split_axis=0,
+            concat_axis=0,
+        ),
+        axis=0,
+    )
     gradient = lax.dot_general(
         columns,
         lax.all_gather(out_grads, "row", axis=0, tiled=True),

time: 270 us -> 268 us (level)
  waiting for transfers between devices: 130 us -> 119 us
  local copies, waits for them, and re-layouts: 6.67 us -> 17 us
    unnamed x9 -> x25, local copies, waits for them, and re-layouts: 4.09 us -> 16.3 us
    all_to_all x1, waiting for transfers between devices: 77.5 us -> 67.7 us  [per_device(): all_to_all(jnp.stack(jnp.split(acts, axis_size('row'), axis=1), axis=0),...]
  transfers between devices with their start and end apart: 2 -> 2, of which waited for: 2 -> 2; matrix products, arithmetic and copies ran while one was open for 4% -> 8% of each run, Pallas kernels for 0% -> 0%
where the time goes in v1:
time: 268 us; the launch traced here: 267 us
  waiting for transfers between devices  119 us (44%)
  blocking collectives  82.2 us (31%)
  local copies, waits for them, and re-layouts  17 us (6%)
  other arithmetic  16.8 us (6%)
  between operations  15.4 us (6%)
  matrix products  9.58 us (4%)
  starting transfers between devices  7.21 us (3%)
    all_to_all x1, waiting for transfers between devices, per_device(): all_to_all(jnp.stack(jnp.split(acts, axis_size('row'), axis=1), axis=0),...  67.7 us
    all_gather x1, waiting for transfers between devices, per_device(): lax.all_gather(out_grads, 'row', axis=0, tiled=True)  50.4 us
    psum x1, blocking collectives, per_device(): update_total = lax.psum(jnp.sum(unclipped * unclipped), ('row', 'col'))  49.2 us
    psum x1, blocking collectives, per_device(): col_total = lax.psum(col_squares, 'row')  30.5 us
    unnamed x25, local copies, waits for them, and re-layouts  16.3 us
    dot_general x1, matrix products, per_device(): lax.dot_general(columns, lax.all_gather(out_grads, 'row', axis=0, tiled=T...  9.58 us
    sub x1, other arithmetic, per_device(): new_weight = weight - step_size * update  8.93 us
    all_to_all x1, starting transfers between devices, per_device(): all_to_all(jnp.stack(jnp.split(acts, axis_size('row'), axis=1), axis=0),...  7.17 us
  transfers between devices with their start and end apart: 2, of which 2 were waited for; matrix products, arithmetic and copies ran while one was open for 8% of the time, Pallas kernels for 0%

profile of v1, /device:TPU:12, one launch (start us, length us, event | category | flops | bytes accessed | tf_op | source)
XLA Modules:
  0.0 267.1 jit_solution(200129442536920540)
XLA Ops:
  7.2 0.7 all-gather.2.cloned.1.call-update
  7.9 1.6 bitcast_dynamic-update-slice_fusion.15
  9.5 1.6 bitcast_dynamic-update-slice_fusion.14
  11.0 1.6 bitcast_dynamic-update-slice_fusion.13
  12.6 1.6 bitcast_dynamic-update-slice_fusion.12
  14.2 1.6 bitcast_dynamic-update-slice_fusion.11
  15.8 1.6 bitcast_dynamic-update-slice_fusion.10
  17.3 1.6 bitcast_dynamic-update-slice_fusion.9
  18.9 0.7 bitcast_dynamic-update-slice_fusion.8
  19.6 0.7 bitcast_dynamic-update-slice_fusion.7
  20.2 0.7 bitcast_dynamic-update-slice_fusion.6
  20.9 0.7 bitcast_dynamic-update-slice_fusion.5
  21.5 0.7 bitcast_dynamic-update-slice_fusion.4
  22.2 0.7 bitcast_dynamic-update-slice_fusion.3
  24.9 7.2 %all-to-all-start = ((bf16[16,128,512]{2,1,0:T(8,128)(2,1)}), bf16[16,128,512]{2,1,0:T(8,128)(2,1)S(1)}, u32[]{:S(2)}, u32[]{:S(2)}) async-start(bf16[16,128,512]{2,1,0:T(8,128)(2,1)} %bitcast_dynamic-update-slice_fusion), calls=%async_computation | async-start | bytes 4194304 | tf_op jit(solution)/shard_map/all_to_all | solution.py:18
  32.0 3.9 %multiply_reduce_fusion.1 = f32[]{:T(128)} fusion(f32[512,2048]{1,0:T(8,128)} %param.7), kind=kLoop, calls=%fused_computation.4 | loop fusion | flops 2097151 | bytes 4194308 | tf_op jit(solution)/shard_map/reduce_sum | solution.py:35
  35.9 67.7 %all-to-all-done = bf16[16,128,512]{2,1,0:T(8,128)(2,1)S(1)} async-done(((bf16[16,128,512]{2,1,0:T(8,128)(2,1)}), bf16[16,128,512]{2,1,0:T(8,128)(2,1)S(1)}, u32[]{:S(2)}, u32[]{:S(2)}) %all-to-all-start) | async-done | bytes 2097184 | tf_op jit(solution)/shard_map/all_to_all | solution.py:18
  103.6 50.4 %all-gather.2.cloned.1.call-done = bf16[2048,2048]{1,0:T(8,128)(2,1)} async-done(((bf16[128,2048]{1,0:T(8,128)(2,1)}), bf16[2048,2048]{1,0:T(8,128)(2,1)}) %all-gather.2.cloned.1.call-update) | async-done | bytes 8388624 | tf_op jit(solution)/shard_map/all_gather | solution.py:28
  154.1 9.6 %fusion.1 = (f32[512]{0:T(512)S(1)}, f32[2048]{0:T(1024)S(1)}, f32[512,2048]{1,0:T(8,128)}) fusion(bf16[2048,512]{1,0:T(8,128)(2,1)S(1)} %bitcast.35, bf16[2048,2048]{1,0:T(8,128)(2,1)} %all-gather.2.cloned.1.call-done), kind=kOutput, calls=%fused_computation.6 | convolution fusion | flops 4299159040 | bytes 14690304 | tf_op jit(solution)/shard_map/dot_general | solution.py:26
  163.6 30.5 %psum.30 = f32[2048]{0:T(1024)S(1)} all-reduce(f32[2048]{0:T(1024)S(1)} %get-tuple-element.5), channel_id=1, replica_groups=mesh['row'=16,'col'=2] {'row'}, use_global_device_ids=true, to_apply=%region_5.0 | all-reduce | flops 2048 | bytes 16384 | tf_op jit(solution)/shard_map/psum | solution.py:37
  194.1 2.5 psum.29
  196.7 4.1 %multiply_reduce_fusion = f32[]{:T(128)} fusion(f32[512,2048]{1,0:T(8,128)} %get-tuple-element.10, f32[2048]{0:T(1024)S(1)} %multiply_add_fusion.1, f32[512]{0:T(512)S(1)} %multiply_add_fusion.2), kind=kLoop, calls=%fused_computation.1 | loop fusion | flops 4194303 | bytes 4204548 | tf_op jit(solution)/shard_map/reduce_sum | solution.py:42
  200.7 49.2 %all-reduce = (f32[]{:T(128)}, f32[]{:T(128)}) all-reduce(f32[]{:T(128)} %multiply_reduce_fusion, f32[]{:T(128)} %multiply_reduce_fusion.1), channel_id=1, replica_groups=mesh['row'=16,'col'=2] {'row','col'}, use_global_device_ids=true, to_apply=%region_7.0 | all-reduce | flops 2 | bytes 16 | tf_op jit(solution)/shard_map/psum | solution.py:42
  251.3 8.9 %multiply_subtract_fusion = (f32[512,2048]{1,0:T(8,128)}, f32[512,2048]{1,0:T(8,128)}) fusion(f32[512,2048]{1,0:T(8,128)} %param.7, f32[]{:T(128)S(6)} %mul_shard_map.3, f32[]{:T(128)S(6)} %max_shard_map.3, f32[512,2048]{1,0:T(8,128)} %get-tuple-element.10, f32[2048]{0:T(1024)S(1)} %multiply_add_fusion.1, f32[512]{0:T(512)S(1)} %multiply_add_fusion.2), kind=kLoop, calls=%fused_computation | loop fusion | flops 5242880 | bytes 16787464 | tf_op jit(solution)/shard_map/sub | solution.py:47
  (16 shorter events, 2.1 us)
Async XLA Ops:
  7.2 11.7 %copy-start = (bf16[128,8192]{1,0:T(8,128)(2,1)S(1)}, bf16[128,8192]{1,0:T(8,128)(2,1)}, u32[]{:S(2)}) copy-start(bf16[128,8192]{1,0:T(8,128)(2,1)} %param.5) | copy-start | bytes 6291460
  7.2 146.9 %all-gather.2.cloned.1.call-start = ((), (), s32[]{:S(2)}) async-start(), calls=%async_computation.1 | async-start | bytes 8912896 | tf_op jit(solution)/shard_map/all_gather | solution.py:28
  24.9 78.7 %all-to-all-start = ((bf16[16,128,512]{2,1,0:T(8,128)(2,1)}), bf16[16,128,512]{2,1,0:T(8,128)(2,1)S(1)}, u32[]{:S(2)}, u32[]{:S(2)}) async-start(bf16[16,128,512]{2,1,0:T(8,128)(2,1)} %bitcast_dynamic-update-slice_fusion), calls=%async_computation | async-start | bytes 4194304 | tf_op jit(solution)/shard_map/all_to_all | solution.py:18
  154.1 42.6 %copy-start.3 = (f32[2048]{0:T(1024)S(1)}, f32[2048]{0:T(1024)}, u32[]{:S(2)}) copy-start(f32[2048]{0:T(1024)} %param.9) | copy-start | bytes 24580
  154.1 42.6 %copy-start.4 = (f32[512]{0:T(512)S(1)}, f32[512]{0:T(512)}, u32[]{:S(2)}) copy-start(f32[512]{0:T(512)} %param.8) | copy-start | bytes 6148
  196.6 54.7 %copy-start.1 = (f32[2048]{0:T(1024)}, f32[2048]{0:T(1024)S(1)}, u32[]{:S(2)}) copy-start(f32[2048]{0:T(1024)S(1)} %multiply_add_fusion.1) | copy-start | bytes 24580
  196.7 54.6 %copy-start.2 = (f32[512]{0:T(512)}, f32[512]{0:T(512)S(1)}, u32[]{:S(2)}) copy-start(f32[512]{0:T(512)S(1)} %multiply_add_fusion.2) | copy-start | bytes 6148
Sparse Core Ops, SparseCore 0:
  10.8 143.2 all-gather.1
